TPU v7x, 32 devices: a whole 2x2x4 slice. The times are simulated.
32 devices in a mesh: ctx: 16 (over z, y, x), fsdp: 2 (over core).
Axes of the slice: x: 2, y: 2, z: 4, core: 2. Of those that a mesh axis runs over, the one named last changes fastest.
Arguments:
- tokens: bfloat16 [2, 2048, 768], P('fsdp', 'ctx'), may hold values from -6 to 6
- cluster_ids: int32 [2, 2048, 12], P('fsdp', 'ctx'), may hold values from 0 to 15, as said below
- qkv_weight: bfloat16 [768, 2304], P('fsdp'), may hold values from -0.21875 to 0.21875
- out_weight: bfloat16 [768, 768], P('fsdp'), may hold values from -2 to 2
- up_weight: bfloat16 [768, 3072], P('fsdp'), may hold values from -0.21875 to 0.21875
- down_weight: bfloat16 [3072, 768], P('fsdp'), may hold values from -0.109375 to 0.109375
- query_bias: float32 [768], P('fsdp'), may hold values from -1 to 1
- value_bias: float32 [768], P('fsdp'), may hold values from -1 to 1
- out_bias: float32 [768], P('fsdp'), may hold values from -1 to 1
- up_bias: float32 [3072], P('fsdp'), may hold values from -1 to 1
- down_bias: float32 [768], P('fsdp'), may hold values from -1 to 1
- first_gain: float32 [768], P('fsdp'), may hold values from 0.25 to 1.75
- first_shift: float32 [768], P('fsdp'), may hold values from -1 to 1
- second_gain: float32 [768], P('fsdp'), may hold values from 0.25 to 1.75
- second_shift: float32 [768], P('fsdp'), may hold values from -1 to 1
- cotangent: bfloat16 [2, 2048, 768], P('fsdp', 'ctx'), may hold values from -6 to 6
Outputs:
- layer_out: bfloat16 [2, 2048, 768], P('fsdp', 'ctx')
- input_grad: bfloat16 [2, 2048, 768], P('fsdp', 'ctx')
- qkv_weight_grad: float32 [768, 2304], P('fsdp')
- out_weight_grad: float32 [768, 768], P('fsdp')
- up_weight_grad: float32 [768, 3072], P('fsdp')
- down_weight_grad: float32 [3072, 768], P('fsdp')
- query_bias_grad: float32 [768], P('fsdp')
- value_bias_grad: float32 [768], P('fsdp')
- out_bias_grad: float32 [768], P('fsdp')
- up_bias_grad: float32 [3072], P('fsdp')
- down_bias_grad: float32 [768], P('fsdp')
- first_gain_grad: float32 [768], P('fsdp')
- first_shift_grad: float32 [768], P('fsdp')
- second_gain_grad: float32 [768], P('fsdp')
- second_shift_grad: float32 [768], P('fsdp')
Inputs may be any that keep to these rules, and one draw needn't show every extreme that they name: `cluster_ids`: for each sequence and head, every cluster id is held by exactly 128 tokens of that sequence.
All inputs are finite; a program needn't handle non-finite values.
Results may differ from a plain program's by a relative error of at most 0.04.
Values may be sent and summed in bfloat16 or wider, within the bound.
No kernel may reach another device: no remote copies, remote signals or barrier semaphores. Data moves between devices by JAX's collectives and lax.ppermute only.
A program may use at most 192 MiB of HBM per device.

v0:
```python
import math

import jax
import jax.numpy as jnp
from jax import lax
from jax.sharding import PartitionSpec as P

HEADS = 12
HEAD_DIM = 64
BLOCK = 256


NEG = -1e30
EPS = 1e-05


def layer_norm(resid, gain, shift):
    center = jnp.mean(resid, axis=-1, keepdims=True)
    centered = resid - center
    spread = jnp.mean(centered * centered, axis=-1, keepdims=True)
    return centered * lax.rsqrt(spread + EPS) * gain + shift


def gelu_exact(value):
    return jax.nn.gelu(value, approximate=False)


def rows_inner(left, right):
    return lax.dot_general(
        left, right, (((0,), (0,)), ((), ())), preferred_element_type=jnp.float32
    )


def times_transposed(left, right):
    return lax.dot_general(
        left, right, (((1,), (1,)), ((), ())), preferred_element_type=jnp.float32
    )


def allowed_mask(query_pos, key_pos, query_ids, key_ids):
    query_block = query_pos // BLOCK
    key_block = key_pos // BLOCK
    same = (query_block[:, None] == key_block[None, :])[:, None, :]
    earlier = (key_block[None, :] < query_block[:, None])[:, None, :]
    match = query_ids[:, :, None] == jnp.transpose(key_ids)[None, :, :]
    return same | earlier & match


def over_rows(step_fn, carry, piece, step):
    count = piece[0].shape[0]

    def turn(index, inner):
        offset = index * step
        part = tuple((lax.dynamic_slice_in_dim(item, offset, step, 0) for item in piece))
        return step_fn(inner, part, offset)

    return lax.fori_loop(0, count // step, turn, carry)


def split_pair(value):
    high_part = value.astype(jnp.bfloat16)
    low_part = (value - high_part.astype(jnp.float32)).astype(jnp.bfloat16)
    return (high_part, low_part)


def per_device(
    tokens,
    cluster_ids,
    qkv_weight,
    out_weight,
    up_weight,
    down_weight,
    query_bias,
    value_bias,
    out_bias,
    up_bias,
    down_bias,
    first_gain,
    first_shift,
    second_gain,
    second_shift,
    cotangent,
):
    scale = 1.0 / math.sqrt(HEAD_DIM)
    shard = (
        qkv_weight,
        out_weight,
        up_weight,
        down_weight,
        query_bias,
        value_bias,
        out_bias,
        up_bias,
        down_bias,
        first_gain,
        first_shift,
        second_gain,
        second_shift,
    )
    gathered = (
        lax.all_gather(shard[0], "fsdp", axis=0, tiled=True),
        lax.all_gather(shard[1], "fsdp", axis=0, tiled=True),
        lax.all_gather(shard[2], "fsdp", axis=0, tiled=True),
        lax.all_gather(shard[3], "fsdp", axis=0, tiled=True),
        lax.all_gather(shard[4].astype(jnp.bfloat16), "fsdp", axis=0, tiled=True).astype(
            jnp.float32
        ),
        lax.all_gather(shard[5].astype(jnp.bfloat16), "fsdp", axis=0, tiled=True).astype(
            jnp.float32
        ),
        lax.all_gather(shard[6].astype(jnp.bfloat16), "fsdp", axis=0, tiled=True).astype(
            jnp.float32
        ),
        lax.all_gather(shard[7].astype(jnp.bfloat16), "fsdp", axis=0, tiled=True).astype(
            jnp.float32
        ),
        lax.all_gather(shard[8].astype(jnp.bfloat16), "fsdp", axis=0, tiled=True).astype(
            jnp.float32
        ),
        lax.all_gather(shard[9].astype(jnp.bfloat16), "fsdp", axis=0, tiled=True).astype(
            jnp.float32
        ),
        lax.all_gather(shard[10].astype(jnp.bfloat16), "fsdp", axis=0, tiled=True).astype(
            jnp.float32
        ),
        lax.all_gather(shard[11].astype(jnp.bfloat16), "fsdp", axis=0, tiled=True).astype(
            jnp.float32
        ),
        lax.all_gather(shard[12].astype(jnp.bfloat16), "fsdp", axis=0, tiled=True).astype(
            jnp.float32
        ),
    )
    qkv_full = gathered[0]
    out_full = gathered[1]
    up_full = gathered[2]
    down_full = gathered[3]
    gain_one = gathered[9]
    gain_two = gathered[11]
    inputs = tokens[0]
    rows = inputs.shape[0]
    width = inputs.shape[1]
    local_ids = cluster_ids[0].astype(jnp.bfloat16)
    positions = lax.axis_index("ctx") * rows + lax.iota(jnp.int32, rows)
    projected = jnp.dot(inputs, qkv_full, preferred_element_type=jnp.float32)
    queries = (projected[:, :width] + gathered[4]).astype(jnp.bfloat16)
    keys = projected[:, width : 2 * width].astype(jnp.bfloat16)
    values = (projected[:, 2 * width :] + gathered[5]).astype(jnp.bfloat16)
    query3 = queries.reshape(rows, HEADS, HEAD_DIM)
    key3 = keys.reshape(rows, HEADS, HEAD_DIM)
    value3 = values.reshape(rows, HEADS, HEAD_DIM)

    def forward_step(carry, piece, start):
        best, total, accum = carry
        key_rows, value_rows, key_ids = piece
        count = key_rows.shape[0]
        piece_keys = key_rows.reshape(count, HEADS, HEAD_DIM)
        piece_values = value_rows.reshape(count, HEADS, HEAD_DIM)
        key_pos = start + lax.iota(jnp.int32, count)
        allowed = allowed_mask(positions, key_pos, local_ids, key_ids)
        scores = (
            jnp.einsum("qhd,khd->qhk", query3, piece_keys, preferred_element_type=jnp.float32)
            * scale
        )
        scores = jnp.where(allowed, scores, NEG)
        fresh = jnp.maximum(best, jnp.max(scores, axis=-1))
        factor = jnp.exp(best - fresh)
        weights = jnp.where(allowed, jnp.exp(scores - fresh[:, :, None]), 0.0)
        total = total * factor + jnp.sum(weights, axis=-1)
        accum = accum * factor[:, :, None] + jnp.einsum(
            "qhk,khd->qhd",
            weights.astype(jnp.bfloat16),
            piece_values,
            preferred_element_type=jnp.float32,
        )
        return (fresh, total, accum)

    start_carry = (
        jnp.full((rows, HEADS), NEG, jnp.float32),
        jnp.zeros((rows, HEADS), jnp.float32),
        jnp.zeros((rows, HEADS, HEAD_DIM), jnp.float32),
    )
    best, total, accum = over_rows(
        forward_step,
        start_carry,
        (
            lax.all_gather(keys, "ctx", axis=0, tiled=True),
            lax.all_gather(values, "ctx", axis=0, tiled=True),
            lax.all_gather(local_ids, "ctx", axis=0, tiled=True),
        ),
        rows,
    )
    attended = (accum / total[:, :, None]).reshape(rows, width)
    log_total = best + jnp.log(total)
    attended_low = attended.astype(jnp.bfloat16)
    branch = jnp.dot(attended_low, out_full, preferred_element_type=jnp.float32) + gathered[6]
    resid_one = inputs.astype(jnp.float32) + branch
    hidden = layer_norm(resid_one, gain_one, gathered[10])
    hidden_low = hidden.astype(jnp.bfloat16)
    pre_act = jnp.dot(hidden_low, up_full, preferred_element_type=jnp.float32) + gathered[7]
    activ_low = gelu_exact(pre_act).astype(jnp.bfloat16)
    ffn = jnp.dot(activ_low, down_full, preferred_element_type=jnp.float32) + gathered[8]
    resid_two = hidden + ffn
    result = layer_norm(resid_two, gain_two, gathered[12])
    again = (
        lax.all_gather(shard[0], "fsdp", axis=0, tiled=True),
        lax.all_gather(shard[1], "fsdp", axis=0, tiled=True),
        lax.all_gather(shard[2], "fsdp", axis=0, tiled=True),
        lax.all_gather(shard[3], "fsdp", axis=0, tiled=True),
        lax.all_gather(shard[4].astype(jnp.bfloat16), "fsdp", axis=0, tiled=True).astype(
            jnp.float32
        ),
        lax.all_gather(shard[5].astype(jnp.bfloat16), "fsdp", axis=0, tiled=True).astype(
            jnp.float32
        ),
        lax.all_gather(shard[6].astype(jnp.bfloat16), "fsdp", axis=0, tiled=True).astype(
            jnp.float32
        ),
        lax.all_gather(shard[7].astype(jnp.bfloat16), "fsdp", axis=0, tiled=True).astype(
            jnp.float32
        ),
        lax.all_gather(shard[8].astype(jnp.bfloat16), "fsdp", axis=0, tiled=True).astype(
            jnp.float32
        ),
        lax.all_gather(shard[9].astype(jnp.bfloat16), "fsdp", axis=0, tiled=True).astype(
            jnp.float32
        ),
        lax.all_gather(shard[10].astype(jnp.bfloat16), "fsdp", axis=0, tiled=True).astype(
            jnp.float32
        ),
        lax.all_gather(shard[11].astype(jnp.bfloat16), "fsdp", axis=0, tiled=True).astype(
            jnp.float32
        ),
        lax.all_gather(shard[12].astype(jnp.bfloat16), "fsdp", axis=0, tiled=True).astype(
            jnp.float32
        ),
    )
    upstream = cotangent[0].astype(jnp.float32)
    norm_two_out, norm_two_back = jax.vjp(layer_norm, resid_two, gain_two, gathered[12])
    grad_two, grad_gain_two, grad_shift_two = norm_two_back(upstream)
    grad_down_bias = jnp.sum(grad_two, axis=0)
    two_low = grad_two.astype(jnp.bfloat16)
    grad_down = rows_inner(activ_low, two_low)
    grad_activ = times_transposed(two_low, again[3])
    gelu_out, gelu_back = jax.vjp(gelu_exact, pre_act)
    grad_pre = gelu_back(grad_activ)[0]
    grad_up_bias = jnp.sum(grad_pre, axis=0)
    pre_low = grad_pre.astype(jnp.bfloat16)
    grad_up = rows_inner(hidden_low, pre_low)
    grad_hidden = grad_two + times_transposed(pre_low, again[2])
    norm_one_out, norm_one_back = jax.vjp(layer_norm, resid_one, gain_one, gathered[10])
    grad_one, grad_gain_one, grad_shift_one = norm_one_back(grad_hidden)
    grad_out_bias = jnp.sum(grad_one, axis=0)
    one_low = grad_one.astype(jnp.bfloat16)
    grad_out = rows_inner(attended_low, one_low)
    grad_att_low = times_transposed(one_low, again[1]).astype(jnp.bfloat16)
    grad3 = grad_att_low.reshape(rows, HEADS, HEAD_DIM)
    delta = jnp.sum(
        (grad_att_low.astype(jnp.float32) * attended).reshape(rows, HEADS, HEAD_DIM), axis=-1
    )
    lse_high, lse_low = split_pair(log_total)
    delta_high, delta_low = split_pair(delta)
    lse_used = lse_high.astype(jnp.float32) + lse_low.astype(jnp.float32)
    delta_used = delta_high.astype(jnp.float32) + delta_low.astype(jnp.float32)

    def query_step(accum_q, piece, start):
        key_rows, value_rows, key_ids = piece
        count = key_rows.shape[0]
        piece_keys = key_rows.reshape(count, HEADS, HEAD_DIM)
        piece_values = value_rows.reshape(count, HEADS, HEAD_DIM)
        key_pos = start + lax.iota(jnp.int32, count)
        allowed = allowed_mask(positions, key_pos, local_ids, key_ids)
        scores = (
            jnp.einsum("qhd,khd->qhk", query3, piece_keys, preferred_element_type=jnp.float32)
            * scale
        )
        probs = jnp.where(allowed, jnp.exp(scores - lse_used[:, :, None]), 0.0)
        dprob = jnp.einsum("qhd,khd->qhk", grad3, piece_values, preferred_element_type=jnp.float32)
        dscore = (probs * (dprob - delta_used[:, :, None])).astype(jnp.bfloat16)
        return accum_q + jnp.einsum(
            "qhk,khd->qhd", dscore, piece_keys, preferred_element_type=jnp.float32
        )

    grad_q3 = over_rows(
        query_step,
        jnp.zeros((rows, HEADS, HEAD_DIM), jnp.float32),
        (
            lax.all_gather(keys, "ctx", axis=0, tiled=True),
            lax.all_gather(values, "ctx", axis=0, tiled=True),
            lax.all_gather(local_ids, "ctx", axis=0, tiled=True),
        ),
        rows,
    )

    def key_step(carry, piece, start):
        grad_k3, grad_v3 = carry
        query_rows, upstream_rows, lse_hi, lse_lo, delta_hi, delta_lo, query_ids = piece
        count = query_rows.shape[0]
        piece_queries = query_rows.reshape(count, HEADS, HEAD_DIM)
        piece_grads = upstream_rows.reshape(count, HEADS, HEAD_DIM)
        query_pos = start + lax.iota(jnp.int32, count)
        allowed = allowed_mask(query_pos, positions, query_ids, local_ids)
        piece_lse = lse_hi.astype(jnp.float32) + lse_lo.astype(jnp.float32)
        piece_delta = delta_hi.astype(jnp.float32) + delta_lo.astype(jnp.float32)
        scores = (
            jnp.einsum("qhd,khd->qhk", piece_queries, key3, preferred_element_type=jnp.float32)
            * scale
        )
        probs = jnp.where(allowed, jnp.exp(scores - piece_lse[:, :, None]), 0.0)
        dprob = jnp.einsum("qhd,khd->qhk", piece_grads, value3, preferred_element_type=jnp.float32)
        dscore = (probs * (dprob - piece_delta[:, :, None])).astype(jnp.bfloat16)
        grad_k3 = grad_k3 + jnp.einsum(
            "qhk,qhd->khd", dscore, piece_queries, preferred_element_type=jnp.float32
        )
        grad_v3 = grad_v3 + jnp.einsum(
            "qhk,qhd->khd",
            probs.astype(jnp.bfloat16),
            piece_grads,
            preferred_element_type=jnp.float32,
        )
        return (grad_k3, grad_v3)

    empty = jnp.zeros((rows, HEADS, HEAD_DIM), jnp.float32)
    grad_k3, grad_v3 = over_rows(
        key_step,
        (empty, empty),
        (
            lax.all_gather(queries, "ctx", axis=0, tiled=True),
            lax.all_gather(grad_att_low, "ctx", axis=0, tiled=True),
            lax.all_gather(lse_high, "ctx", axis=0, tiled=True),
            lax.all_gather(lse_low, "ctx", axis=0, tiled=True),
            lax.all_gather(delta_high, "ctx", axis=0, tiled=True),
            lax.all_gather(delta_low, "ctx", axis=0, tiled=True),
            lax.all_gather(local_ids, "ctx", axis=0, tiled=True),
        ),
        rows,
    )
    query_grad_low = (grad_q3 * scale).reshape(rows, width).astype(jnp.bfloat16)
    key_grad_low = (grad_k3 * scale).reshape(rows, width).astype(jnp.bfloat16)
    value_grad_low = grad_v3.reshape(rows, width).astype(jnp.bfloat16)
    qkv_grad_low = jnp.concatenate([query_grad_low, key_grad_low, value_grad_low], axis=1)
    grad_qkv = rows_inner(inputs, qkv_grad_low)
    grad_query_bias = jnp.sum(query_grad_low.astype(jnp.float32), axis=0)
    grad_value_bias = jnp.sum(value_grad_low.astype(jnp.float32), axis=0)
    grad_input = (grad_one + times_transposed(qkv_grad_low, again[0])).astype(jnp.bfloat16)
    grads = (
        grad_qkv,
        grad_out,
        grad_up,
        grad_down,
        grad_query_bias,
        grad_value_bias,
        grad_out_bias,
        grad_up_bias,
        grad_down_bias,
        grad_gain_one,
        grad_shift_one,
        grad_gain_two,
        grad_shift_two,
    )
    summed = lax.psum(
        (
            grads[0],
            grads[1],
            grads[2],
            grads[3],
            grads[4],
            grads[5],
            grads[6],
            grads[7],
            grads[8],
            grads[9],
            grads[10],
            grads[11],
            grads[12],
        ),
        "ctx",
    )
    halves = (
        lax.psum_scatter(
            summed[0].astype(jnp.bfloat16), "fsdp", scatter_dimension=0, tiled=True
        ).astype(jnp.float32),
        lax.psum_scatter(
            summed[1].astype(jnp.bfloat16), "fsdp", scatter_dimension=0, tiled=True
        ).astype(jnp.float32),
        lax.psum_scatter(
            summed[2].astype(jnp.bfloat16), "fsdp", scatter_dimension=0, tiled=True
        ).astype(jnp.float32),
        lax.psum_scatter(
            summed[3].astype(jnp.bfloat16), "fsdp", scatter_dimension=0, tiled=True
        ).astype(jnp.float32),
        lax.psum_scatter(
            summed[4].astype(jnp.bfloat16), "fsdp", scatter_dimension=0, tiled=True
        ).astype(jnp.float32),
        lax.psum_scatter(
            summed[5].astype(jnp.bfloat16), "fsdp", scatter_dimension=0, tiled=True
        ).astype(jnp.float32),
        lax.psum_scatter(
            summed[6].astype(jnp.bfloat16), "fsdp", scatter_dimension=0, tiled=True
        ).astype(jnp.float32),
        lax.psum_scatter(
            summed[7].astype(jnp.bfloat16), "fsdp", scatter_dimension=0, tiled=True
        ).astype(jnp.float32),
        lax.psum_scatter(
            summed[8].astype(jnp.bfloat16), "fsdp", scatter_dimension=0, tiled=True
        ).astype(jnp.float32),
        lax.psum_scatter(
            summed[9].astype(jnp.bfloat16), "fsdp", scatter_dimension=0, tiled=True
        ).astype(jnp.float32),
        lax.psum_scatter(
            summed[10].astype(jnp.bfloat16), "fsdp", scatter_dimension=0, tiled=True
        ).astype(jnp.float32),
        lax.psum_scatter(
            summed[11].astype(jnp.bfloat16), "fsdp", scatter_dimension=0, tiled=True
        ).astype(jnp.float32),
        lax.psum_scatter(
            summed[12].astype(jnp.bfloat16), "fsdp", scatter_dimension=0, tiled=True
        ).astype(jnp.float32),
    )
    return (
        result.astype(jnp.bfloat16)[None],
        grad_input[None],
        halves[0],
        halves[1],
        halves[2],
        halves[3],
        halves[4],
        halves[5],
        halves[6],
        halves[7],
        halves[8],
        halves[9],
        halves[10],
        halves[11],
        halves[12],
    )


def solution(mesh):
    placed = (
        P("fsdp", "ctx", None),
        P("fsdp", "ctx", None),
        P("fsdp", None),
        P("fsdp", None),
        P("fsdp", None),
        P("fsdp", None),
        P("fsdp"),
        P("fsdp"),
        P("fsdp"),
        P("fsdp"),
        P("fsdp"),
        P("fsdp"),
        P("fsdp"),
        P("fsdp"),
        P("fsdp"),
        P("fsdp", "ctx", None),
    )
    return jax.shard_map(
        per_device,
        mesh=mesh,
        in_specs=placed,
        out_specs=(
            P("fsdp", "ctx", None),
            P("fsdp", "ctx", None),
            P("fsdp", None),
            P("fsdp", None),
            P("fsdp", None),
            P("fsdp", None),
            P("fsdp"),
            P("fsdp"),
            P("fsdp"),
            P("fsdp"),
            P("fsdp"),
            P("fsdp"),
            P("fsdp"),
            P("fsdp"),
            P("fsdp"),
        ),
        check_vma=False,
    )
```

profile of v0, /device:TPU:0, one launch (start us, length us, event | category | flops | bytes accessed | tf_op | source)
XLA Modules:
  0.0 1791.8 jit_solution(8541714317696250311)
XLA Ops:
  8.0 17.0 all-gather.19.cloned.1.call-done
  25.0 2.6 fusion.83
  52.5 43.8 %all-gather = bf16[1,2048,12]{1,2,0:T(8,128)(2,1)} all-gather(bf16[1,128,12]{1,2,0:T(8,128)(2,1)S(1)} %copy_convert_fusion), channel_id=2, replica_groups=mesh['ctx'=16,'fsdp'=2] {'ctx'}, dimensions={1}, use_global_device_ids=true | all-gather | bytes 52224 | tf_op jit(solution)/shard_map/all_gather | solution.py:188
  98.9 4.6 copy.64
  103.6 64.9 %all-gather.23.cloned.1.call-done = bf16[2048,768]{1,0:T(8,128)(2,1)} async-done(((bf16[128,768]{1,0:T(8,128)(2,1)}), bf16[2048,768]{1,0:T(8,128)(2,1)}) %all-gather.23.cloned.1.call-update) | async-done | bytes 3145744 | tf_op jit(solution)/shard_map/all_gather | solution.py:187
  168.5 4.6 copy.65
  173.1 66.7 %while.63 = (s32[]{:T(128)}, f32[128,12]{0,1:T(8,128)S(1)}, f32[128,12]{0,1:T(8,128)S(1)}, f32[128,12,64]{0,2,1:T(8,128)S(1)}, bf16[128,12]{0,1:T(8,128)(2,1)S(1...) while((s32[]{:T(128)}, f32[128,12]{0,1:T(8,128)S(1)}, ...), condition=%wide.region_3.4_spmd.clone.clone.clone, body=%wide.region_0.3_spmd.clone.clone.clone.sunk | while | flops 55389828 | bytes 4778199 | solution.py:57
  243.4 8.4 multiply_convert_fusion
  251.9 3.6 fusion.106
  257.5 2.5 fusion.107
  268.1 60.8 %while.64 = (s32[]{:T(128)}, f32[128,12,64]{0,2,1:T(8,128)S(1)}, bf16[2048,768]{0,1:T(8,128)(2,1)}, bf16[128,12]{0,1:T(8,128)(2,1)}, bf16[2048,12]{0,1:T(8,128)(...) while((s32[]{:T(128)}, f32[128,12,64]{0,2,1:T(8,128)S(1)}, ...), condition=%wide.region_14.15_spmd.clone.clone.clone, body=%wide.region_13.14_spmd.clone.clone.clone.sunk | while | flops 77893760 | bytes 4221149 | solution.py:57
  328.9 3.1 fusion.85
  332.1 5.2 fusion.77
  337.3 5.1 fusion.95
  344.6 38.8 %all_gather.91 = bf16[2048,12]{0,1:T(8,128)(2,1)S(1)} all-gather(bf16[128,12]{0,1:T(8,128)(2,1)S(1)} %copy-done.36), channel_id=1, replica_groups=mesh['ctx'=16,'fsdp'=2] {'ctx'}, dimensions={0}, use_global_device_ids=true | all-gather | bytes 52224 | tf_op jit(solution)/shard_map/all_gather | solution.py:329
  383.4 35.8 %all_gather.92 = bf16[2048,12]{0,1:T(8,128)(2,1)S(1)} all-gather(bf16[128,12]{0,1:T(8,128)(2,1)S(1)} %copy-done.35), channel_id=1, replica_groups=mesh['ctx'=16,'fsdp'=2] {'ctx'}, dimensions={0}, use_global_device_ids=true | all-gather | bytes 52224 | tf_op jit(solution)/shard_map/all_gather | solution.py:330
  419.2 37.8 %all_gather.94 = bf16[2048,12]{0,1:T(8,128)(2,1)S(1)} all-gather(bf16[128,12]{0,1:T(8,128)(2,1)S(1)} %copy-done.34), channel_id=1, replica_groups=mesh['ctx'=16,'fsdp'=2] {'ctx'}, dimensions={0}, use_global_device_ids=true | all-gather | bytes 52224 | tf_op jit(solution)/shard_map/all_gather | solution.py:331
  456.9 35.8 %all_gather.95 = bf16[2048,12]{0,1:T(8,128)(2,1)S(1)} all-gather(bf16[128,12]{0,1:T(8,128)(2,1)S(1)} %get-tuple-element.1631), channel_id=1, replica_groups=mesh['ctx'=16,'fsdp'=2] {'ctx'}, dimensions={0}, use_global_device_ids=true | all-gather | bytes 52224 | tf_op jit(solution)/shard_map/all_gather | solution.py:332
  492.8 74.5 %while.65 = (s32[]{:T(128)}, f32[128,12,64]{0,2,1:T(8,128)S(1)}, f32[128,12,64]{0,2,1:T(8,128)S(1)}, bf16[2048,768]{1,0:T(8,128)(2,1)}, bf16[2048,12]{0,1:T(8,12...) while((s32[]{:T(128)}, f32[128,12,64]{0,2,1:T(8,128)S(1)}, ...), condition=%wide.region_16.17_spmd.clone.clone.clone, body=%wide.region_15.16_spmd.clone.clone.clone.sunk | while | flops 103462016 | bytes 6801658 | solution.py:57
  567.4 4.0 convolution_bitcast_fusion.4
  571.5 1131.5 %all-reduce.12 = (bf16[768,2304]{0,1:T(8,128)(2,1)}, bf16[768,768]{1,0:T(8,128)(2,1)}, bf16[768,3072]{1,0:T(8,128)(2,1)}, bf16[3072,768]{1,0:T(8,128)(2,1)}, bf1...) all-reduce(f32[768,2304]{0,1:T(8,128)} %convolution_bitcast_fusion., ...), channel_id=1, replica_groups=mesh['ctx'=16,'fsdp'=2] {'ctx'}, use_global_device_ids=true, to_apply=%region_17.18 | all-reduce | flops 7087104 | bytes 42522624 | tf_op jit(solution)/shard_map/psum | solution.py:360
  1703.1 5.7 copy.78
  1712.2 3.7 all-reduce.10
  1721.8 4.0 fusion.68
  1725.8 6.9 reduce-scatter.7.cloned.1.call-done
  1734.8 13.2 reduce-scatter.13.cloned.1.call-done
  1748.0 2.8 copy.79
  1750.7 2.7 copy.75
  1753.5 11.2 reduce-scatter.9.cloned.1.call-done
  1764.7 4.4 convert_element_type.380
  1769.1 11.6 reduce-scatter.11.cloned.1.call-done
  1780.7 4.2 convert_element_type.382
  (676 shorter events, 252.5 us)
Async XLA Ops:
  7.2 17.8 copy-start.9
  7.2 17.8 all-gather.19.cloned.1.call-start
  7.9 20.5 %copy-start.48 = (f32[384]{0:T(512)S(1)}, f32[384]{0:T(512)}, u32[]{:S(2)}) copy-start(f32[384]{0:T(512)} %param.29) | copy-start | bytes 4612
  7.9 22.3 %copy-start.49 = (f32[384]{0:T(512)S(1)}, f32[384]{0:T(512)}, u32[]{:S(2)}) copy-start(f32[384]{0:T(512)} %param.28) | copy-start | bytes 4612
  7.9 91.0 %all-gather.21.cloned.1.call-start = ((), (), s32[]{:S(2)}) async-start(), calls=%async_computation.5 | async-start | bytes 3342336 | tf_op jit(solution)/shard_map/all_gather | solution.py:186
  28.4 140.1 %all-gather.23.cloned.1.call-start = ((), (), s32[]{:S(2)}) async-start(), calls=%async_computation.6 | async-start | bytes 3342336 | tf_op jit(solution)/shard_map/all_gather | solution.py:187
  32.9 65.0 %copy-start.12 = (bf16[128,768]{1,0:T(8,128)(2,1)}, bf16[128,768]{1,0:T(8,128)(2,1)S(1)}, u32[]{:S(2)}) copy-start(bf16[128,768]{1,0:T(8,128)(2,1)S(1)} %get-tuple-element.1628) | copy-start | bytes 589828
  32.9 207.0 %all-gather.25.cloned.1.call-start = ((), (), s32[]{:S(2)}) async-start(), calls=%async_computation.7 | async-start | bytes 1769472 | tf_op jit(solution)/shard_map/all_gather | solution.py:102
  33.5 209.5 %all-gather.27.cloned.1.call-start = ((), (), s32[]{:S(2)}) async-start(), calls=%async_computation.8 | async-start | bytes 7077888 | tf_op jit(solution)/shard_map/all_gather | solution.py:103
  34.1 10.5 copy-start.53
  34.1 12.9 copy-start.54
  34.1 15.3 copy-start.55
  34.1 17.7 copy-start.11
  34.1 18.3 %copy-start.26 = (s32[1,128,12]{1,0,2:T(1,128)S(1)}, s32[1,128,12]{1,0,2:T(1,128)}, u32[]{:S(2)}) copy-start(s32[1,128,12]{1,0,2:T(1,128)} %param.23) | copy-start | bytes 18436
  34.2 62.7 %copy-start.13 = (bf16[128,768]{1,0:T(8,128)(2,1)S(1)}, bf16[128,768]{1,0:T(8,128)(2,1)}, u32[]{:S(2)}) copy-start(bf16[128,768]{1,0:T(8,128)(2,1)} %slice.23) | copy-start | bytes 589828
  34.2 63.5 %copy-start.14 = (bf16[128,768]{1,0:T(8,128)(2,1)S(1)}, bf16[128,768]{1,0:T(8,128)(2,1)}, u32[]{:S(2)}) copy-start(bf16[128,768]{1,0:T(8,128)(2,1)} %get-tuple-element.1627) | copy-start | bytes 589828
  34.2 217.7 %all-gather.29.cloned.1.call-start = ((), (), s32[]{:S(2)}) async-start(), calls=%async_computation.9 | async-start | bytes 7077888 | tf_op jit(solution)/shard_map/all_gather | solution.py:104
  34.8 458.0 %all-gather.31.cloned.1.call-start = ((), (), s32[]{:S(2)}) async-start(), calls=%async_computation.10 | async-start | bytes 3342336 | tf_op jit(solution)/shard_map/all_gather | solution.py:327
  98.7 394.1 %all-gather.33.cloned.1.call-start = ((), (), s32[]{:S(2)}) async-start(), calls=%async_computation.11 | async-start | bytes 3342336 | tf_op jit(solution)/shard_map/all_gather | solution.py:328
  103.6 69.5 %copy-start.21 = (bf16[128,12]{0,1:T(8,128)(2,1)S(1)}, bf16[128,12]{0,1:T(8,128)(2,1)}, u32[]{:S(2)}) copy-start(bf16[128,12]{0,1:T(8,128)(2,1)} %fusion.134) | copy-start | bytes 9220
  173.1 66.8 %copy-start.32 = (f32[768]{0:T(1024)S(1)}, f32[768]{0:T(1024)}, u32[]{:S(2)}) copy-start(f32[768]{0:T(1024)} %reshape.596) | copy-start | bytes 9220
  266.0 1466.6 %reduce-scatter.7.cloned.1.call-start = ((), (), s32[]{:S(2)}) async-start(), calls=%async_computation.12 | async-start | bytes 1769472 | tf_op jit(solution)/shard_map/reduce_scatter | solution.py:382
  268.0 60.8 %copy-start.43 = (f32[128]{0:T(128)S(1)}, f32[128]{0:T(128)}, u32[]{:S(2)}) copy-start(f32[128]{0:T(128)} %copy-done.42) | copy-start | bytes 1540
  337.3 46.1 %copy-start.35 = (bf16[128,12]{0,1:T(8,128)(2,1)S(1)}, bf16[128,12]{0,1:T(8,128)(2,1)}, u32[]{:S(2)}) copy-start(bf16[128,12]{0,1:T(8,128)(2,1)} %get-tuple-element.1597) | copy-start | bytes 9220
  337.3 81.9 %copy-start.34 = (bf16[128,12]{0,1:T(8,128)(2,1)S(1)}, bf16[128,12]{0,1:T(8,128)(2,1)}, u32[]{:S(2)}) copy-start(bf16[128,12]{0,1:T(8,128)(2,1)} %get-tuple-element.1632) | copy-start | bytes 9220
  342.4 150.4 %copy-start.22 = (bf16[128,12]{0,1:T(8,128)(2,1)S(1)}, bf16[128,12]{0,1:T(8,128)(2,1)}, u32[]{:S(2)}) copy-start(bf16[128,12]{0,1:T(8,128)(2,1)} %get-tuple-element.2100) | copy-start | bytes 9220
  492.7 74.7 %copy-start.10 = (bf16[1,128,768]{2,1,0:T(8,128)(2,1)S(1)}, bf16[1,128,768]{2,1,0:T(8,128)(2,1)}, u32[]{:S(2)}) copy-start(bf16[1,128,768]{2,1,0:T(8,128)(2,1)} %param.22) | copy-start | bytes 589828
  492.8 74.7 %copy-start.17 = (bf16[128,12,64]{0,2,1:T(8,128)(2,1)S(1)}, bf16[128,12,64]{0,2,1:T(8,128)(2,1)}, u32[]{:S(2)}) copy-start(bf16[128,12,64]{0,2,1:T(8,128)(2,1)} %get-tuple-element.1595) | copy-start | bytes 589828
  1703.1 44.9 %reduce-scatter.13.cloned.1.call-start = ((), (), s32[]{:S(2)}) async-start(), calls=%async_computation.15 | async-start | bytes 5308416
  1708.9 55.7 %reduce-scatter.9.cloned.1.call-start = ((), (), s32[]{:S(2)}) async-start(), calls=%async_computation.13 | async-start | bytes 7077888 | tf_op jit(solution)/shard_map/reduce_scatter | solution.py:385
  1709.6 71.1 %reduce-scatter.11.cloned.1.call-start = ((), (), s32[]{:S(2)}) async-start(), calls=%async_computation.14 | async-start | bytes 7077888 | tf_op jit(solution)/shard_map/reduce_scatter | solution.py:388
  1709.7 12.1 copy-start.45
  (45 other events, 176.6 us)
Sparse Core Ops, SparseCore 0:
  9.6 15.3 all-gather.18
  28.5 69.6 all-gather.20
  101.5 66.8 all-gather.22
  169.9 7.7 all-gather.24
  179.0 15.5 all-gather.26
  196.0 15.6 all-gather.28
  214.5 69.4 all-gather.30
  287.3 66.5 all-gather.32
  1703.2 29.3 reduce-scatter.6
  1735.4 12.5 reduce-scatter.12
  1750.8 13.7 reduce-scatter.8
  1766.9 13.7 reduce-scatter.10
where the time goes:
time: 1800 us; the launch traced here: 1790 us
  blocking collectives  1340 us (74%)
  matrix products  143 us (8%)
  waiting for transfers between devices  128 us (7%)
  local copies, waits for them, and re-layouts  122 us (7%)
  other arithmetic  35.2 us (2%)
    psum x1, blocking collectives, per_device(): lax.psum((grads[0], grads[1], grads[2], grads[3], grads[4], grads[5], gra...  1130 us
    dynamic_slice x96, local copies, waits for them, and re-layouts, turn(): lax.dynamic_slice_in_dim(item, offset, step, 0)  67.3 us
    all_gather x1, waiting for transfers between devices, per_device(): lax.all_gather(values, 'ctx', axis=0, tiled=True)  64.9 us
    all_gather x1, blocking collectives, per_device(): lax.all_gather(local_ids, 'ctx', axis=0, tiled=True)  43.8 us
    all_gather x1, blocking collectives, per_device(): lax.all_gather(lse_high, 'ctx', axis=0, tiled=True)  38.8 us
    all_gather x1, blocking collectives, per_device(): lax.all_gather(delta_high, 'ctx', axis=0, tiled=True)  37.8 us
  transfers between devices with their start and end apart: 12, of which 6 were waited for; matrix products, arithmetic and copies ran while one was open for 12% of the time, Pallas kernels for 0%

commit v1 on v0

v1 whole, which is shorter than its diff:
```python
import functools
import math

import jax
import jax.numpy as jnp
from jax import lax
from jax.experimental import pallas as pl
from jax.experimental.pallas import tpu as pltpu
from jax.sharding import PartitionSpec as P

HEADS = 12
HEAD_DIM = 64
BLOCK = 256
CLUSTER = 128
EPS = 1e-05
FEAT = 128
FAR = 2.0**100
F32 = jnp.float32
BF = jnp.bfloat16


def dot(a,b): return jnp.dot(a,b,preferred_element_type=F32)
def dot_nt(a,b): return lax.dot_general(a,b,(((1,),(1,)),((),())),preferred_element_type=F32)

def fwd_body(x_ref, o_ref, full_ref, lse_ref, qf_ref, kf_ref, vt_ref):
    pieces, rows_in, rows = x_ref.shape
    length = pieces*rows
    clusters = length // 128
    nb = length // BLOCK
    def build(j, _):
        at = pl.ds(pl.multiple_of(j*rows, rows), rows)
        q = x_ref[j, 0:64, :]; k = x_ref[j, 64:128, :]; v = x_ref[j,128:192,:]
        ids = x_ref[j, 192:200, :].astype(F32)[0:1, :]
        row = lax.broadcasted_iota(jnp.int32, (FEAT-HEAD_DIM, rows), 0).astype(F32)
        same = row == ids
        qf_ref[:, at] = jnp.concatenate([q, same.astype(F32).astype(BF)], axis=0)
        far = jnp.where(same, 0.0, -FAR).astype(BF)
        kf_ref[at, :] = jnp.concatenate([k, far], axis=0).T
        vt_ref[:, at] = v
        return 0
    lax.fori_loop(0, pieces, build, 0)
    def qstep(qb, _):
        qat = pl.ds(pl.multiple_of(qb*BLOCK, BLOCK), BLOCK)
        q = qf_ref[:, qat]
        s = dot(kf_ref[qat, 0:HEAD_DIM], q[0:HEAD_DIM])
        m = jnp.max(s, axis=0, keepdims=True)
        p = jnp.exp(s-m)
        l = jnp.sum(p, axis=0, keepdims=True)
        acc = dot(vt_ref[:, qat], p.astype(BF))
        def kstep(kb, c):
            m,l,acc = c
            kat = pl.ds(pl.multiple_of(kb*BLOCK, BLOCK), BLOCK)
            s = dot(kf_ref[kat,:], q)
            m2 = jnp.maximum(m, jnp.max(s,axis=0,keepdims=True))
            a = jnp.exp(m-m2); p = jnp.exp(s-m2)
            l = l*a + jnp.sum(p,axis=0,keepdims=True)
            acc = acc*a + dot(vt_ref[:,kat], p.astype(BF))
            return m2,l,acc
        m,l,acc = lax.fori_loop(0, qb, kstep, (m,l,acc))
        o = acc / l
        full_ref[:, qat] = o
        lse_ref[:, qat] = m + jnp.log(l)
        ob = o.astype(BF)
        for t in range(BLOCK//rows):
            o_ref[qb*(BLOCK//rows)+t] = ob[:, t*rows:(t+1)*rows]
        return 0
    lax.fori_loop(0, nb, qstep, 0)

def attn_fwd(x):
    pieces, _, rows = x.shape; length=pieces*rows
    outs = (jax.ShapeDtypeStruct((pieces,HEAD_DIM,rows),BF), jax.ShapeDtypeStruct((HEAD_DIM,length),F32),
            jax.ShapeDtypeStruct((1,length),F32), jax.ShapeDtypeStruct((FEAT,length),BF), jax.ShapeDtypeStruct((length,FEAT),BF), jax.ShapeDtypeStruct((HEAD_DIM,length),BF))
    return pl.pallas_call(fwd_body, out_shape=outs,
        in_specs=[pl.BlockSpec(memory_space=pltpu.VMEM)], out_specs=tuple(pl.BlockSpec(memory_space=pltpu.VMEM) for _ in outs),
        compiler_params=pltpu.CompilerParams(vmem_limit_bytes=48<<20), name="attention_forward")(x)

def bwd_body(x_ref, g_ref, full_ref, lse_ref, qf_ref, kf_ref, vt_ref, out_ref, gt_ref, delta_ref, v_ref, kt_ref, dk_ref, dv_ref):
    pieces, rows_in, rows = x_ref.shape
    length = pieces*rows
    nb = length // BLOCK
    def build(j, _):
        at = pl.ds(pl.multiple_of(j*rows, rows), rows)
        g = g_ref[j]
        gt_ref[:, at] = g
        delta_ref[:, at] = jnp.sum(g.astype(F32)*full_ref[:, at], axis=0, keepdims=True)
        v_ref[at,:] = x_ref[j,128:192,:].T
        kt_ref[:, at] = x_ref[j,64:128,:]
        return 0
    lax.fori_loop(0, pieces, build, 0)
    def block(kat, qat, feats, first):
        q = qf_ref[0:feats, qat]
        lse = lse_ref[:, qat]
        g = gt_ref[:, qat]
        s = dot(kf_ref[kat,0:feats], q)
        p = jnp.exp(s - lse)
        dp = dot(v_ref[kat,:], g)
        ds = (p*(dp - delta_ref[:, qat])).astype(BF)
        dv = dot_nt(g, p.astype(BF))
        dk = dot_nt(q[0:HEAD_DIM], ds)
        if first:
            dv_ref[:,kat] = dv; dk_ref[:,kat] = dk
        else:
            dv_ref[:,kat] += dv; dk_ref[:,kat] += dk
        return dot(kt_ref[:,kat], ds)
    def qstep(qb, _):
        qat = pl.ds(pl.multiple_of(qb*BLOCK, BLOCK), BLOCK)
        dq = block(qat, qat, HEAD_DIM, True)
        def kstep(kb, dq):
            kat = pl.ds(pl.multiple_of(kb*BLOCK, BLOCK), BLOCK)
            return dq + block(kat, qat, FEAT, False)
        dq = lax.fori_loop(0, qb, kstep, dq)
        dqb = (dq*(1.0/math.sqrt(HEAD_DIM))).astype(BF)
        for t in range(BLOCK//rows):
            out_ref[qb*(BLOCK//rows)+t, 0:64, :] = dqb[:, t*rows:(t+1)*rows]
        return 0
    lax.fori_loop(0, nb, qstep, 0)
    def finish(j, _):
        at = pl.ds(pl.multiple_of(j*rows, rows), rows)
        out_ref[j, 64:128, :] = dk_ref[:, at].astype(BF)
        out_ref[j, 128:192, :] = dv_ref[:, at].astype(BF)
        return 0
    lax.fori_loop(0, pieces, finish, 0)

def attn_bwd(x, g, full, lse, qf, kf, vt):
    pieces, _, rows = x.shape; length=pieces*rows
    return pl.pallas_call(bwd_body, out_shape=jax.ShapeDtypeStruct((pieces,3*HEAD_DIM,rows),BF),
        in_specs=[pl.BlockSpec(memory_space=pltpu.VMEM)]*7, out_specs=pl.BlockSpec(memory_space=pltpu.VMEM),
        scratch_shapes=[pltpu.VMEM((HEAD_DIM,length),BF), pltpu.VMEM((1,length),F32), pltpu.VMEM((length,HEAD_DIM),BF), pltpu.VMEM((HEAD_DIM,length),BF),
            pltpu.VMEM((HEAD_DIM,length),F32), pltpu.VMEM((HEAD_DIM,length),F32)],
        compiler_params=pltpu.CompilerParams(vmem_limit_bytes=48<<20), name="attention_backward")(x,g,full,lse,qf,kf,vt)


def layer_norm(resid, gain, shift):
    center = jnp.mean(resid, axis=-1, keepdims=True)
    centered = resid - center
    spread = jnp.mean(centered * centered, axis=-1, keepdims=True)
    return centered * lax.rsqrt(spread + EPS) * gain + shift


def gelu_exact(value):
    return jax.nn.gelu(value, approximate=False)


def contract(left, right, left_dim, right_dim):
    return lax.dot_general(
        left, right, (((left_dim,), (right_dim,)), ((), ())), preferred_element_type=F32
    )


def swap(value):
    return lax.ppermute(value, "fsdp", [(0, 1), (1, 0)])


def half_of(value, index, axis):
    size = value.shape[axis] // 2
    return lax.dynamic_slice_in_dim(value, index * size, size, axis)


def exchange(value, bit, count):
    return lax.ppermute(value, "ctx", [(i, i ^ (1 << bit)) for i in range(count)])


def split_axis(shape):
    if (shape[0] // 2) % 16 == 0:
        return 0
    if (shape[1] // 2) % 128 == 0:
        return 1
    return 0


def reduce_scatter(value, order, count, index):
    axes = []
    for bit in order:
        axis = split_axis(value.shape)
        axes.append(axis)
        mine = (index >> bit) & 1
        arrived = exchange(half_of(value, 1 - mine, axis), bit, count)
        value = (half_of(value, mine, axis).astype(F32) + arrived.astype(F32)).astype(BF)
    return value, axes


def gather_back(value, order, axes, count, index):
    for bit, axis in zip(reversed(order), reversed(axes)):
        arrived = exchange(value, bit, count)
        mine = (index >> bit) & 1
        value = jnp.where(
            mine == 0,
            jnp.concatenate([value, arrived], axis),
            jnp.concatenate([arrived, value], axis),
        )
    return value


def sum_over_tokens(value, cuts, orders, count, index):
    pieces = []
    start = 0
    for size, order in zip(cuts, orders):
        part, axes = reduce_scatter(value[:, start : start + size], order, count, index)
        pieces.append(gather_back(part, order, axes, count, index))
        start += size
    return jnp.concatenate(pieces, 1).astype(F32)


def per_device(
    count,
    tokens,
    cluster_ids,
    qkv_weight,
    out_weight,
    up_weight,
    down_weight,
    query_bias,
    value_bias,
    out_bias,
    up_bias,
    down_bias,
    first_gain,
    first_shift,
    second_gain,
    second_shift,
    cotangent,
):
    side = lax.axis_index("fsdp")
    place = lax.axis_index("ctx")
    other = 1 - side
    vectors = (
        query_bias,
        value_bias,
        out_bias,
        up_bias,
        down_bias,
        first_gain,
        first_shift,
        second_gain,
        second_shift,
    )
    sizes = [item.shape[0] for item in vectors]
    starts = [sum(sizes[:i]) for i in range(len(sizes) + 1)]
    qkv_other = swap(qkv_weight)
    packed = jnp.concatenate(vectors)
    packed_other = swap(packed)
    out_other, up_other, down_other = swap(out_weight), swap(up_weight), swap(down_weight)
    low_half = jnp.where(side == 0, packed, packed_other)
    high_half = jnp.where(side == 0, packed_other, packed)

    def whole(i):
        return jnp.concatenate(
            [low_half[starts[i] : starts[i + 1]], high_half[starts[i] : starts[i + 1]]]
        )

    bias_q, bias_v, bias_out, bias_up, bias_down, gain_one, shift_one, gain_two, shift_two = (
        whole(i) for i in range(9)
    )
    inputs = tokens[0]
    rows, width = inputs.shape
    slots = -(-HEADS // count) * count
    per = slots // count
    scale = 1.0 / math.sqrt(HEAD_DIM)

    in_mine, in_other = half_of(inputs, side, 1), half_of(inputs, other, 1)
    projected = contract(qkv_weight, in_mine, 0, 1) + contract(qkv_other, in_other, 0, 1)
    queries = ((projected[:width] + bias_q[:, None]) * scale).astype(BF)
    keys = projected[width : 2 * width].astype(BF)
    values = (projected[2 * width :] + bias_v[:, None]).astype(BF)
    ids = jnp.transpose(cluster_ids[0]).astype(BF)
    chunks = jnp.concatenate(
        [
            queries.reshape(HEADS, HEAD_DIM, rows),
            keys.reshape(HEADS, HEAD_DIM, rows),
            values.reshape(HEADS, HEAD_DIM, rows),
            jnp.broadcast_to(ids[:, None, :], (HEADS, 8, rows)),
        ],
        axis=1,
    )
    chunks = jnp.pad(chunks, ((0, slots - HEADS), (0, 0), (0, 0)))

    def to_heads(value):
        return lax.all_to_all(
            value.reshape(count, per, *value.shape[1:]), "ctx", 0, 0, tiled=False
        )

    def to_tokens(value):
        arrived = lax.all_to_all(value, "ctx", 0, 0, tiled=False)
        return arrived.reshape(slots, *arrived.shape[2:])[:HEADS]

    gathered = to_heads(chunks)
    kept = [attn_fwd(gathered[:, i]) for i in range(per)]
    attended = to_tokens(jnp.stack([item[0] for item in kept], 1)).reshape(width, rows)
    att_mine, att_other = half_of(attended, side, 0), half_of(attended, other, 0)
    branch = contract(att_mine, out_weight, 0, 0) + contract(att_other, out_other, 0, 0)
    resid_one = inputs.astype(F32) + branch + bias_out
    hidden = layer_norm(resid_one, gain_one, shift_one)
    hidden_low = hidden.astype(BF)
    hid_mine, hid_other = half_of(hidden_low, side, 1), half_of(hidden_low, other, 1)
    pre_act = (
        contract(hid_mine, up_weight, 1, 0) + contract(hid_other, up_other, 1, 0) + bias_up
    )
    activ_low = gelu_exact(pre_act).astype(BF)
    act_mine, act_other = half_of(activ_low, side, 1), half_of(activ_low, other, 1)
    ffn = (
        contract(act_mine, down_weight, 1, 0) + contract(act_other, down_other, 1, 0) + bias_down
    )
    resid_two = hidden + ffn
    upstream = cotangent[0].astype(F32)
    result, norm_two_back = jax.vjp(layer_norm, resid_two, gain_two, shift_two)
    grad_two, grad_gain_two, grad_shift_two = norm_two_back(upstream)
    two_low = grad_two.astype(BF)

    def in_order(mine, others):
        return jnp.where(
            side == 0,
            jnp.concatenate([mine, others], 1),
            jnp.concatenate([others, mine], 1),
        )

    grad_activ = in_order(contract(two_low, down_weight, 1, 1), contract(two_low, down_other, 1, 1))
    gelu_back = jax.vjp(gelu_exact, pre_act)[1]
    grad_pre = gelu_back(grad_activ)[0]
    pre_low = grad_pre.astype(BF)
    grad_hidden = grad_two + in_order(
        contract(pre_low, up_weight, 1, 1), contract(pre_low, up_other, 1, 1)
    )
    norm_one_back = jax.vjp(layer_norm, resid_one, gain_one, shift_one)[1]
    grad_one, grad_gain_one, grad_shift_one = norm_one_back(grad_hidden)
    one_low = grad_one.astype(BF)
    to_out_mine = contract(out_weight, one_low, 1, 1)
    to_out_other = contract(out_other, one_low, 1, 1)
    grad_att = jnp.where(
        side == 0,
        jnp.concatenate([to_out_mine, to_out_other], 0),
        jnp.concatenate([to_out_other, to_out_mine], 0),
    ).astype(BF)
    grad_chunks = jnp.pad(
        grad_att.reshape(HEADS, HEAD_DIM, rows), ((0, slots - HEADS), (0, 0), (0, 0))
    )
    grad_heads = to_heads(grad_chunks)

    def both(mine, theirs, axis=0):
        return jnp.concatenate([mine, swap(theirs)], axis)

    grad_down = contract(both(act_mine, act_other), both(two_low, two_low), 0, 0).astype(BF)
    grad_up = contract(both(hid_mine, hid_other), both(pre_low, pre_low), 0, 0).astype(BF)
    grad_out = contract(both(att_mine, att_other, 1), both(one_low, one_low), 1, 0).astype(BF)

    backs = []
    for i in range(per):
        _, full, lse, feat_q, feat_k, val = kept[i]
        backs.append(attn_bwd(gathered[:, i], grad_heads[:, i], full, lse, feat_q, feat_k, val))
    grad_qkv_low = to_tokens(jnp.stack(backs, 1))
    grad_qkv_low = grad_qkv_low.reshape(HEADS, 3, HEAD_DIM, rows)
    grad_qkv_low = jnp.transpose(grad_qkv_low, (1, 0, 2, 3)).reshape(3 * width, rows)
    grad_qkv = contract(
        both(in_mine, in_other), both(grad_qkv_low, grad_qkv_low, 1), 0, 1
    ).astype(BF)
    grad_input = (
        grad_one
        + in_order(
            contract(grad_qkv_low, qkv_weight, 0, 1), contract(grad_qkv_low, qkv_other, 0, 1)
        )
    ).astype(BF)

    small = (
        jnp.sum(grad_qkv_low[:width].astype(F32), axis=1),
        jnp.sum(grad_qkv_low[2 * width :].astype(F32), axis=1),
        jnp.sum(grad_one, axis=0),
        jnp.sum(grad_pre, axis=0),
        jnp.sum(grad_two, axis=0),
        grad_gain_one,
        grad_shift_one,
        grad_gain_two,
        grad_shift_two,
    )
    small_halves = jnp.concatenate([item.reshape(2, -1) for item in small], 1)
    small_mine = half_of(small_halves, side, 0) + swap(half_of(small_halves, other, 0))
    small_mine = small_mine.reshape(-1, 128)
    bits = list(range(count.bit_length() - 1))
    for bit in bits:
        small_mine = small_mine + exchange(small_mine, bit, count)
    small_mine = small_mine.reshape(-1)
    first = bits
    second = [bits[1], bits[0]] + bits[2:]
    third = bits[2:] + bits[:2]
    summed = (
        sum_over_tokens(grad_qkv, (896, 896, 512), (first, second, third), count, place),
        sum_over_tokens(grad_out, (768,), (third,), count, place),
        sum_over_tokens(grad_up, (2304, 768), (second, third), count, place),
        sum_over_tokens(grad_down, (512, 256), (first, third), count, place),
    )
    return (
        result.astype(BF)[None],
        grad_input[None],
        *summed,
        *(small_mine[starts[i] : starts[i + 1]] for i in range(9)),
    )


def solution(mesh):
    matrix = P("fsdp", None)
    vector = P("fsdp")
    rows = P("fsdp", "ctx", None)
    return jax.shard_map(
        functools.partial(per_device, mesh.shape["ctx"]),
        mesh=mesh,
        in_specs=(rows, rows) + (matrix,) * 4 + (vector,) * 9 + (rows,),
        out_specs=(rows, rows) + (matrix,) * 4 + (vector,) * 9,
        check_vma=False,
    )
```

time: 1800 us -> 410 us (0.23)
  blocking collectives: 1340 us -> 0 us
  starting transfers between devices: 0.88 us -> 116 us
  matrix products: 143 us -> 36.6 us
  local copies, waits for them, and re-layouts: 122 us -> 33 us
  Pallas kernels: 0 us -> 33 us
  waiting for transfers between devices: 128 us -> 156 us
    psum x1 -> x0, blocking collectives: 1130 us -> none  [per_device(): lax.psum((grads[0], grads[1], grads[2], grads[3], grads[4], grads[5], gra...]
    all_gather x14 -> x0, blocking collectives: 208 us -> none  [the longest x1 43.8 us: per_device(): lax.all_gather(local_ids, 'ctx', axis=0, tiled=True)]
    ppermute x0 -> x82, waiting for transfers between devices: none -> 131 us  [the longest x68 130 us: exchange(): return lax.ppermute(value, 'ctx', [(i, i ^ 1 << bit) for i in range(count)])]
    dot_general x124 -> x20, matrix products: 143 us -> 36.6 us  [contract(): lax.dot_general(left, right, (((left_dim,), (right_dim,)), ((), ())), pre...]
    ppermute x0 -> x82, starting transfers between devices: none -> 94.6 us  [the longest x68 91.3 us: exchange(): return lax.ppermute(value, 'ctx', [(i, i ^ 1 << bit) for i in range(count)])]
    all_gather x8 -> x0, waiting for transfers between devices: 82 us -> none  [the longest x1 64.9 us: per_device(): lax.all_gather(values, 'ctx', axis=0, tiled=True)]
    dynamic_slice x96 -> x37, local copies, waits for them, and re-layouts: 67.3 us -> 6.83 us  [half_of(): return lax.dynamic_slice_in_dim(value, index * size, size, axis)]
    pallas_call x0 -> x2, Pallas kernels: none -> 33 us  [the longest x1 16.6 us: attn_bwd(): pl.pallas_call(bwd_body, out_shape=jax.ShapeDtypeStruct((pieces, 3 * HEAD...]
  transfers between devices with their start and end apart: 12 -> 86, of which waited for: 6 -> 39; matrix products, arithmetic and copies ran while one was open for 12% -> 23% of each run, Pallas kernels for 0% -> 8%
where the time goes in v1:
time: 410 us; the launch traced here: 408 us
  waiting for transfers between devices  156 us (38%)
  starting transfers between devices  116 us (28%)
  matrix products  36.6 us (9%)
  local copies, waits for them, and re-layouts  33 us (8%)
  Pallas kernels  33 us (8%)
  other arithmetic  31.6 us (8%)
    ppermute x68, waiting for transfers between devices, exchange(): return lax.ppermute(value, 'ctx', [(i, i ^ 1 << bit) for i in range(count)])  130 us
    ppermute x68, starting transfers between devices, exchange(): return lax.ppermute(value, 'ctx', [(i, i ^ 1 << bit) for i in range(count)])  91.3 us
    dot_general x20, matrix products, contract(): lax.dot_general(left, right, (((left_dim,), (right_dim,)), ((), ())), pre...  36.6 us
    all_to_all x2, waiting for transfers between devices, to_heads(): lax.all_to_all(value.reshape(count, per, *value.shape[1:]), 'ctx', 0, 0,...  18.7 us
    pallas_call x1, Pallas kernels, attn_bwd(): pl.pallas_call(bwd_body, out_shape=jax.ShapeDtypeStruct((pieces, 3 * HEAD...  16.6 us
    pallas_call x1, Pallas kernels, attn_fwd(): pl.pallas_call(fwd_body, out_shape=outs, in_specs=[pl.BlockSpec(memory_sp...  16.4 us
    all_to_all x2, starting transfers between devices, to_heads(): lax.all_to_all(value.reshape(count, per, *value.shape[1:]), 'ctx', 0, 0,...  11.8 us
    unnamed x79, local copies, waits for them, and re-layouts  11.7 us
  transfers between devices with their start and end apart: 86, of which 39 were waited for; matrix products, arithmetic and copies ran while one was open for 23% of the time, Pallas kernels for 8%

profile of v1, /device:TPU:0, one launch (start us, length us, event | category | flops | bytes accessed | tf_op | source)
XLA Modules:
  0.0 408.1 jit_solution(13490037651947696486)
XLA Ops:
  14.8 8.3 %all-to-all-start = ((bf16[16,1,200,128]{3,2,1,0:T(8,128)(2,1)}), bf16[16,1,200,128]{3,2,1,0:T(8,128)(2,1)S(1)}, u32[]{:S(2)}, u32[]{:S(2)}) async-start(bf16[16,1,200,128]{3,2,1,0:T(8,128)(2,1)} %fusion.25), calls=%async_computation | async-start | bytes 1638400 | tf_op jit(solution)/shard_map/all_to_all | solution.py:278
  24.9 18.7 %all-to-all-done = bf16[16,1,200,128]{3,2,1,0:T(8,128)(2,1)S(1)} async-done(((bf16[16,1,200,128]{3,2,1,0:T(8,128)(2,1)}), bf16[16,1,200,128]{3,2,1,0:T(8,128)(2,1)S(1)}, u32[]{:S(2)}, u32[]{:S(2)}) %all-to-all-start) | async-done | bytes 819232 | tf_op jit(solution)/shard_map/all_to_all | solution.py:278
  43.6 16.4 %attention_forward.1 = (bf16[16,64,128]{2,1,0:T(8,128)(2,1)}, f32[64,2048]{1,0:T(8,128)S(1)}, f32[1,2048]{1,0:T(1,128)S(1)}, bf16[128,2048]{1,0:T(8,128)(2,1)S(1...) custom-call(bf16[16,200,128]{2,1,0:T(8,128)(2,1)S(1)} %bitcast.119), custom_call_target="tpu_custom_call" | custom-call | tf_op jit(solution)/shard_map/attention_forward/pallas_call | solution.py:73
  60.1 5.1 %all-to-all-start.1 = ((bf16[16,1,64,128]{3,2,1,0:T(8,128)(2,1)}), bf16[16,1,64,128]{3,2,1,0:T(8,128)(2,1)}, u32[]{:S(2)}, u32[]{:S(2)}) async-start(bf16[16,1,64,128]{3,2,1,0:T(8,128)(2,1)} %bitcast.12), calls=%async_computation.1 | async-start | bytes 524288 | tf_op jit(solution)/shard_map/all_to_all | solution.py:283
  67.0 6.7 %all-to-all-done.1 = bf16[16,1,64,128]{3,2,1,0:T(8,128)(2,1)} async-done(((bf16[16,1,64,128]{3,2,1,0:T(8,128)(2,1)}), bf16[16,1,64,128]{3,2,1,0:T(8,128)(2,1)}, u32[]{:S(2)}, u32[]{:S(2)}) %all-to-all-start.1) | async-done | bytes 262176 | tf_op jit(solution)/shard_map/all_to_all | solution.py:283
  80.4 5.2 %multiply_convert_fusion = (bf16[128,3072]{1,0:T(8,128)(2,1)S(1)}, f32[128,3072]{1,0:T(8,128)S(1)}, f32[128,3072]{1,0:T(8,128)S(1)}) fusion(f32[3072]{0:T(1024)S(1)} %copy-done.26, f32[128,3072]{1,0:T(8,128)S(1)} %fusion.81, bf16[128,384]{1,0:T(8,128)(2,1)} %get-tuple-element.54, bf16[384,3072]{1,0:T(8,128)(2,1)} %collective-permute-done.3), kind=kOutput, calls=%fused_computation.26 | convolution fusion | flops 328335360 | bytes 7974912 | tf_op jit(solution)/shard_map/dot_general | solution.py:145
  93.3 2.6 fusion.83
  95.8 2.6 fusion.84
  99.8 2.8 fusion.85
  119.2 3.5 all-to-all-start.2
  124.0 2.8 collective-permute-start.34
  128.9 9.4 %collective-permute-done.34 = bf16[96,768]{1,0:T(8,128)(2,1)S(1)} collective-permute-done((bf16[96,768]{1,0:T(8,128)(2,1)S(1)}, bf16[96,768]{1,0:T(8,128)(2,1)S(1)}, u32[]{:S(2)}, u32[]{:S(2)}) %collective-permute-start.34) | collective-permute-done | bytes 147488 | tf_op jit(solution)/shard_map/ppermute | solution.py:160
  140.1 2.6 collective-permute-done.35
  145.8 16.6 %attention_backward.1 = bf16[16,192,128]{2,1,0:T(8,128)(2,1)} custom-call(bf16[16,200,128]{2,1,0:T(8,128)(2,1)S(1)} %bitcast.120, bf16[16,64,128]{2,1,0:T(8,128)(2,1)S(1)} %bitcast.121, f32[64,2048]{1,0:T(8,128)S(1)} %get-tuple-element.22.full_ref, f32[1,2048]{1,0:T(1,128)S(1)} %get-tuple-element.23.lse_ref, bf16[128,2048]{1,0:T(8,128)(2,1)S(1)} %get-tuple-element.24.qf_ref, ...), custom_call_target="tpu_custom_call" | custom-call | tf_op jit(solution)/shard_map/attention_backward/pallas_call | solution.py:126
  162.4 4.1 all-to-all-start.3
  179.2 14.8 %collective-permute-done.38 = bf16[48,768]{1,0:T(8,128)(2,1)S(1)} collective-permute-done((bf16[48,768]{1,0:T(8,128)(2,1)S(1)}, bf16[48,768]{1,0:T(8,128)(2,1)S(1)}, u32[]{:S(2)}, u32[]{:S(2)}) %collective-permute-start.38) | collective-permute-done | bytes 73760 | tf_op jit(solution)/shard_map/ppermute | solution.py:160
  199.5 3.2 collective-permute-done.71
  203.4 10.5 %collective-permute-done.72 = bf16[96,256]{1,0:T(8,128)(2,1)S(1)} collective-permute-done((bf16[96,256]{1,0:T(8,128)(2,1)S(1)}, bf16[96,256]{1,0:T(8,128)(2,1)S(1)}, u32[]{:S(2)}, u32[]{:S(2)}) %collective-permute-start.72) | collective-permute-done | bytes 49184 | tf_op jit(solution)/shard_map/ppermute | solution.py:160
  213.9 2.8 collective-permute-start.52
  225.4 3.0 collective-permute-done.53
  230.0 2.9 collective-permute-done.54
  235.1 6.0 %collective-permute-done.55 = bf16[48,384]{1,0:T(8,128)(2,1)S(1)} collective-permute-done((bf16[48,384]{1,0:T(8,128)(2,1)S(1)}, bf16[48,384]{1,0:T(8,128)(2,1)S(1)}, u32[]{:S(2)}, u32[]{:S(2)}) %collective-permute-start.55) | collective-permute-done | bytes 36896 | tf_op jit(solution)/shard_map/ppermute | solution.py:160
  256.6 8.4 %collective-permute-done.63 = bf16[192,512]{1,0:T(8,128)(2,1)S(1)} collective-permute-done((bf16[192,512]{1,0:T(8,128)(2,1)S(1)}, bf16[192,512]{1,0:T(8,128)(2,1)S(1)}, u32[]{:S(2)}, u32[]{:S(2)}) %collective-permute-start.63) | collective-permute-done | bytes 196640 | tf_op jit(solution)/shard_map/ppermute | solution.py:160
  268.2 3.5 collective-permute-done.64
  295.3 2.6 collective-permute-start.81
  304.4 3.5 collective-permute-done.45
  312.5 4.6 %collective-permute-done.46 = bf16[48,1152]{1,0:T(8,128)(2,1)S(1)} collective-permute-done((bf16[48,1152]{1,0:T(8,128)(2,1)S(1)}, bf16[48,1152]{1,0:T(8,128)(2,1)S(1)}, u32[]{:S(2)}, u32[]{:S(2)}) %collective-permute-start.46) | collective-permute-done | bytes 110624 | tf_op jit(solution)/shard_map/ppermute | solution.py:160
  329.3 4.1 %collective-permute-done.24 = bf16[96,512]{1,0:T(8,128)(2,1)S(1)} collective-permute-done((bf16[96,512]{1,0:T(8,128)(2,1)S(1)}, bf16[96,512]{1,0:T(8,128)(2,1)S(1)}, u32[]{:S(2)}, u32[]{:S(2)}) %collective-permute-start.24) | collective-permute-done | bytes 98336 | tf_op jit(solution)/shard_map/ppermute | solution.py:160
  335.7 15.6 %collective-permute-done.25 = bf16[48,512]{1,0:T(8,128)(2,1)S(1)} collective-permute-done((bf16[48,512]{1,0:T(8,128)(2,1)S(1)}, bf16[48,512]{1,0:T(8,128)(2,1)S(1)}, u32[]{:S(2)}, u32[]{:S(2)}) %collective-permute-start.25) | collective-permute-done | bytes 49184 | tf_op jit(solution)/shard_map/ppermute | solution.py:160
  366.9 4.6 %collective-permute-done.29 = bf16[96,512]{1,0:T(8,128)(2,1)S(1)} collective-permute-done((bf16[96,512]{1,0:T(8,128)(2,1)S(1)}, bf16[96,512]{1,0:T(8,128)(2,1)S(1)}, u32[]{:S(2)}, u32[]{:S(2)}) %collective-permute-start.29) | collective-permute-done | bytes 98336 | tf_op jit(solution)/shard_map/ppermute | solution.py:160
  399.6 2.9 collective-permute-done.14
  405.3 2.8 maximum_convert_fusion
  (418 shorter events, 202.8 us)
Async XLA Ops:
  14.8 28.8 %all-to-all-start = ((bf16[16,1,200,128]{3,2,1,0:T(8,128)(2,1)}), bf16[16,1,200,128]{3,2,1,0:T(8,128)(2,1)S(1)}, u32[]{:S(2)}, u32[]{:S(2)}) async-start(bf16[16,1,200,128]{3,2,1,0:T(8,128)(2,1)} %fusion.25), calls=%async_computation | async-start | bytes 1638400 | tf_op jit(solution)/shard_map/all_to_all | solution.py:278
  23.1 294.1 %collective-permute-start.5 = (bf16[128,384]{1,0:T(8,128)(2,1)}, bf16[128,384]{1,0:T(8,128)(2,1)}, u32[]{:S(2)}, u32[]{:S(2)}) collective-permute-start(bf16[128,384]{1,0:T(8,128)(2,1)} %get-tuple-element.58), channel_id=1, source_target_pairs={{0,1},{1,0},{2,3},{3,2},{4,5},{5,4},{6,7},{7,6},{8,9},{9,8},{10,11... | collective-permute-start | bytes 294920 | tf_op jit(solution)/shard_map/ppermute | solution.py:151
  23.2 51.9 %collective-permute-start.2 = (bf16[384,768]{1,0:T(8,128)(2,1)S(1)}, bf16[384,768]{1,0:T(8,128)(2,1)}, u32[]{:S(2)}, u32[]{:S(2)}) collective-permute-start(bf16[384,768]{1,0:T(8,128)(2,1)S(1)} %copy-done.12), channel_id=1, source_target_pairs={{0,1},{1,0},{2,3},{3,2},{4,5},{5,4},{6,7},{7,6},{8,9},{9,8},{10,11... | collective-permute-start | bytes 1769480 | tf_op jit(solution)/shard_map/ppermute | solution.py:151
  23.7 56.7 %collective-permute-start.3 = (bf16[384,3072]{1,0:T(8,128)(2,1)}, bf16[384,3072]{1,0:T(8,128)(2,1)}, u32[]{:S(2)}, u32[]{:S(2)}) collective-permute-start(bf16[384,3072]{1,0:T(8,128)(2,1)} %param.20), channel_id=1, source_target_pairs={{0,1},{1,0},{2,3},{3,2},{4,5},{5,4},{6,7},{7,6},{8,9},{9,8},{10,11... | collective-permute-start | bytes 7077896 | tf_op jit(solution)/shard_map/ppermute | solution.py:151
  23.8 65.0 %collective-permute-start.4 = (bf16[1536,768]{1,0:T(8,128)(2,1)}, bf16[1536,768]{1,0:T(8,128)(2,1)}, u32[]{:S(2)}, u32[]{:S(2)}) collective-permute-start(bf16[1536,768]{1,0:T(8,128)(2,1)} %param.21), channel_id=1, source_target_pairs={{0,1},{1,0},{2,3},{3,2},{4,5},{5,4},{6,7},{7,6},{8,9},{9,8},{10,11... | collective-permute-start | bytes 7077896 | tf_op jit(solution)/shard_map/ppermute | solution.py:151
  74.8 32.8 %collective-permute-start.31 = (bf16[384,128]{1,0:T(8,128)(2,1)S(1)}, bf16[384,128]{1,0:T(8,128)(2,1)S(1)}, u32[]{:S(2)}, u32[]{:S(2)}) collective-permute-start(bf16[384,128]{1,0:T(8,128)(2,1)S(1)} %get-tuple-element.56), channel_id=1, source_target_pairs={{0,1},{1,0},{2,3},{3,2},{4,5},{5,4},{6,7},{7,6},{8,9},{9,8},{10,11... | collective-permute-start | bytes 294920 | tf_op jit(solution)/shard_map/ppermute | solution.py:151
  77.6 91.9 %collective-permute-start.41 = (bf16[128,384]{1,0:T(8,128)(2,1)}, bf16[128,384]{1,0:T(8,128)(2,1)}, u32[]{:S(2)}, u32[]{:S(2)}) collective-permute-start(bf16[128,384]{1,0:T(8,128)(2,1)} %get-tuple-element.54), channel_id=1, source_target_pairs={{0,1},{1,0},{2,3},{3,2},{4,5},{5,4},{6,7},{7,6},{8,9},{9,8},{10,11... | collective-permute-start | bytes 294920 | tf_op jit(solution)/shard_map/ppermute | solution.py:151
  86.5 40.3 %collective-permute-start.59 = (bf16[128,1536]{1,0:T(8,128)(2,1)}, bf16[128,1536]{1,0:T(8,128)(2,1)}, u32[]{:S(2)}, u32[]{:S(2)}) collective-permute-start(bf16[128,1536]{1,0:T(8,128)(2,1)} %get-tuple-element.47), channel_id=1, source_target_pairs={{0,1},{1,0},{2,3},{3,2},{4,5},{5,4},{6,7},{7,6},{8,9},{9,8},{10,11... | collective-permute-start | bytes 1179656 | tf_op jit(solution)/shard_map/ppermute | solution.py:151
  119.2 26.6 %all-to-all-start.2 = ((bf16[16,1,64,128]{3,2,1,0:T(8,128)(2,1)}), bf16[16,1,64,128]{3,2,1,0:T(8,128)(2,1)S(1)}, u32[]{:S(2)}, u32[]{:S(2)}) async-start(bf16[16,1,64,128]{3,2,1,0:T(8,128)(2,1)} %pad_bitcast_fusion), calls=%async_computation.2 | async-start | bytes 524288 | tf_op jit(solution)/shard_map/all_to_all | solution.py:278
  122.7 48.4 %collective-permute-start.42 = (bf16[128,3072]{1,0:T(8,128)(2,1)}, bf16[128,3072]{1,0:T(8,128)(2,1)}, u32[]{:S(2)}, u32[]{:S(2)}) collective-permute-start(bf16[128,3072]{1,0:T(8,128)(2,1)} %copy-done.3), channel_id=1, source_target_pairs={{0,1},{1,0},{2,3},{3,2},{4,5},{5,4},{6,7},{7,6},{8,9},{9,8},{10,11... | collective-permute-start | bytes 2359304 | tf_op jit(solution)/shard_map/ppermute | solution.py:151
  140.0 35.5 %collective-permute-start.69 = (bf16[768,256]{1,0:T(8,128)(2,1)S(1)}, bf16[768,256]{1,0:T(8,128)(2,1)}, u32[]{:S(2)}, u32[]{:S(2)}) collective-permute-start(bf16[768,256]{1,0:T(8,128)(2,1)S(1)} %constant_dynamic-slice_fusion.5), channel_id=1, source_target_pairs={{0,8},{2,10},{4,12},{6,14},{8,0},{10,2},{12,4},{14,6},{16,24},{18,... | collective-permute-start | bytes 1179656 | tf_op jit(solution)/shard_map/ppermute | solution.py:160
  143.4 23.1 %collective-permute-start.36 = (bf16[48,384]{1,0:T(8,128)(2,1)}, bf16[48,384]{1,0:T(8,128)(2,1)S(1)}, u32[]{:S(2)}, u32[]{:S(2)}) collective-permute-start(bf16[48,384]{1,0:T(8,128)(2,1)} %constant_dynamic-slice_fusion.18), channel_id=1, source_target_pairs={{0,4},{2,6},{4,0},{6,2},{8,12},{10,14},{12,8},{14,10},{16,20},{18,... | collective-permute-start | bytes 110600 | tf_op jit(solution)/shard_map/ppermute | solution.py:160
  162.4 111.6 %all-to-all-start.3 = ((bf16[16,1,192,128]{3,2,1,0:T(8,128)(2,1)}), bf16[16,1,192,128]{3,2,1,0:T(8,128)(2,1)S(1)}, u32[]{:S(2)}, u32[]{:S(2)}) async-start(bf16[16,1,192,128]{3,2,1,0:T(8,128)(2,1)} %bitcast.23), calls=%async_computation.3 | async-start | bytes 1572864 | tf_op jit(solution)/shard_map/all_to_all | solution.py:283
  167.1 56.7 %collective-permute-start.61 = (bf16[768,512]{1,0:T(8,128)(2,1)}, bf16[768,512]{1,0:T(8,128)(2,1)S(1)}, u32[]{:S(2)}, u32[]{:S(2)}) collective-permute-start(bf16[768,512]{1,0:T(8,128)(2,1)} %constant_dynamic-slice_fusion.9), channel_id=1, source_target_pairs={{0,2},{2,0},{4,6},{6,4},{8,10},{10,8},{12,14},{14,12},{16,18},{18,... | collective-permute-start | bytes 2359304 | tf_op jit(solution)/shard_map/ppermute | solution.py:160
  173.4 24.6 %collective-permute-start.51 = (bf16[192,768]{1,0:T(8,128)(2,1)S(1)}, bf16[192,768]{1,0:T(8,128)(2,1)S(1)}, u32[]{:S(2)}, u32[]{:S(2)}) collective-permute-start(bf16[192,768]{1,0:T(8,128)(2,1)S(1)} %constant_dynamic-slice_fusion.13), channel_id=1, source_target_pairs={{0,8},{2,10},{4,12},{6,14},{8,0},{10,2},{12,4},{14,6},{16,24},{18,... | collective-permute-start | bytes 884744 | tf_op jit(solution)/shard_map/ppermute | solution.py:160
  174.9 19.0 %collective-permute-start.38 = (bf16[48,768]{1,0:T(8,128)(2,1)S(1)}, bf16[48,768]{1,0:T(8,128)(2,1)S(1)}, u32[]{:S(2)}, u32[]{:S(2)}) collective-permute-start(bf16[48,768]{1,0:T(8,128)(2,1)S(1)} %maximum_select_fusion.33), channel_id=1, source_target_pairs={{0,2},{2,0},{4,6},{6,4},{8,10},{10,8},{12,14},{14,12},{16,18},{18,... | collective-permute-start | bytes 221192 | tf_op jit(solution)/shard_map/ppermute | solution.py:160
  176.7 18.8 %collective-permute-start.70 = (bf16[384,256]{1,0:T(8,128)(2,1)S(1)}, bf16[384,256]{1,0:T(8,128)(2,1)S(1)}, u32[]{:S(2)}, u32[]{:S(2)}) collective-permute-start(bf16[384,256]{1,0:T(8,128)(2,1)S(1)} %constant_dynamic-slice_fusion.4), channel_id=1, source_target_pairs={{0,16},{2,18},{4,20},{6,22},{8,24},{10,26},{12,28},{14,30},{16,0},... | collective-permute-start | bytes 589832 | tf_op jit(solution)/shard_map/ppermute | solution.py:160
  194.0 62.4 %collective-permute-start.43 = (bf16[192,2304]{1,0:T(8,128)(2,1)S(1)}, bf16[192,2304]{1,0:T(8,128)(2,1)S(1)}, u32[]{:S(2)}, u32[]{:S(2)}) collective-permute-start(bf16[192,2304]{1,0:T(8,128)(2,1)S(1)} %constant_dynamic-slice_fusion.17), channel_id=1, source_target_pairs={{0,4},{2,6},{4,0},{6,2},{8,12},{10,14},{12,8},{14,10},{16,20},{18,... | collective-permute-start | bytes 2654216 | tf_op jit(solution)/shard_map/ppermute | solution.py:160
  195.5 21.2 %collective-permute-start.39 = (bf16[96,768]{1,0:T(8,128)(2,1)S(1)}, bf16[96,768]{1,0:T(8,128)(2,1)S(1)}, u32[]{:S(2)}, u32[]{:S(2)}) collective-permute-start(bf16[96,768]{1,0:T(8,128)(2,1)S(1)} %maximum_select_fusion.27), channel_id=1, source_target_pairs={{0,16},{2,18},{4,20},{6,22},{8,24},{10,26},{12,28},{14,30},{16,0},... | collective-permute-start | bytes 442376 | tf_op jit(solution)/shard_map/ppermute | solution.py:160
  220.9 21.7 %collective-permute-start.40 = (bf16[192,768]{1,0:T(8,128)(2,1)S(1)}, bf16[192,768]{1,0:T(8,128)(2,1)S(1)}, u32[]{:S(2)}, u32[]{:S(2)}) collective-permute-start(bf16[192,768]{1,0:T(8,128)(2,1)S(1)} %maximum_select_fusion.19), channel_id=1, source_target_pairs={{0,8},{2,10},{4,12},{6,14},{8,0},{10,2},{12,4},{14,6},{16,24},{18,... | collective-permute-start | bytes 884744 | tf_op jit(solution)/shard_map/ppermute | solution.py:160
  232.9 18.0 %collective-permute-start.62 = (bf16[384,512]{1,0:T(8,128)(2,1)S(1)}, bf16[384,512]{1,0:T(8,128)(2,1)S(1)}, u32[]{:S(2)}, u32[]{:S(2)}) collective-permute-start(bf16[384,512]{1,0:T(8,128)(2,1)S(1)} %constant_dynamic-slice_fusion.8), channel_id=1, source_target_pairs={{0,4},{2,6},{4,0},{6,2},{8,12},{10,14},{12,8},{14,10},{16,20},{18,... | collective-permute-start | bytes 1179656 | tf_op jit(solution)/shard_map/ppermute | solution.py:160
  249.6 23.2 %collective-permute-start.76 = (bf16[768,256]{1,0:T(8,128)(2,1)S(1)}, bf16[768,256]{1,0:T(8,128)(2,1)S(1)}, u32[]{:S(2)}, u32[]{:S(2)}) collective-permute-start(bf16[768,256]{1,0:T(8,128)(2,1)S(1)} %maximum_select_fusion.16), channel_id=1, source_target_pairs={{0,8},{2,10},{4,12},{6,14},{8,0},{10,2},{12,4},{14,6},{16,24},{18,... | collective-permute-start | bytes 1179656 | tf_op jit(solution)/shard_map/ppermute | solution.py:160
  253.8 28.7 %collective-permute-start.58 = (bf16[192,768]{1,0:T(8,128)(2,1)S(1)}, bf16[192,768]{1,0:T(8,128)(2,1)}, u32[]{:S(2)}, u32[]{:S(2)}) collective-permute-start(bf16[192,768]{1,0:T(8,128)(2,1)S(1)} %maximum_select_fusion.20), channel_id=1, source_target_pairs={{0,8},{2,10},{4,12},{6,14},{8,0},{10,2},{12,4},{14,6},{16,24},{18,... | collective-permute-start | bytes 884744 | tf_op jit(solution)/shard_map/ppermute | solution.py:160
  267.3 33.5 %collective-permute-start.44 = (bf16[96,2304]{1,0:T(8,128)(2,1)}, bf16[96,2304]{1,0:T(8,128)(2,1)}, u32[]{:S(2)}, u32[]{:S(2)}) collective-permute-start(bf16[96,2304]{1,0:T(8,128)(2,1)} %constant_dynamic-slice_fusion.16), channel_id=1, source_target_pairs={{0,2},{2,0},{4,6},{6,4},{8,10},{10,8},{12,14},{14,12},{16,18},{18,... | collective-permute-start | bytes 1327112 | tf_op jit(solution)/shard_map/ppermute | solution.py:160
  272.4 25.6 %collective-permute-start.65 = (bf16[96,512]{1,0:T(8,128)(2,1)}, bf16[96,512]{1,0:T(8,128)(2,1)}, u32[]{:S(2)}, u32[]{:S(2)}) collective-permute-start(bf16[96,512]{1,0:T(8,128)(2,1)} %add_convert_fusion.22), channel_id=1, source_target_pairs={{0,16},{2,18},{4,20},{6,22},{8,24},{10,26},{12,28},{14,30},{16,0},... | collective-permute-start | bytes 294920 | tf_op jit(solution)/shard_map/ppermute | solution.py:160
  285.6 31.7 %collective-permute-start.6 = (bf16[2304,128]{1,0:T(8,128)(2,1)S(1)}, bf16[2304,128]{1,0:T(8,128)(2,1)S(1)}, u32[]{:S(2)}, u32[]{:S(2)}) collective-permute-start(bf16[2304,128]{1,0:T(8,128)(2,1)S(1)} %bitcast.123), channel_id=1, source_target_pairs={{0,1},{1,0},{2,3},{3,2},{4,5},{5,4},{6,7},{7,6},{8,9},{9,8},{10,11... | collective-permute-start | bytes 1769480 | tf_op jit(solution)/shard_map/ppermute | solution.py:151
  321.6 31.0 %collective-permute-start.15 = (bf16[192,896]{1,0:T(8,128)(2,1)S(1)}, bf16[192,896]{1,0:T(8,128)(2,1)S(1)}, u32[]{:S(2)}, u32[]{:S(2)}) collective-permute-start(bf16[192,896]{1,0:T(8,128)(2,1)S(1)} %constant_dynamic-slice_fusion.29), channel_id=1, source_target_pairs={{0,4},{2,6},{4,0},{6,2},{8,12},{10,14},{12,8},{14,10},{16,20},{18,... | collective-permute-start | bytes 1032200 | tf_op jit(solution)/shard_map/ppermute | solution.py:160
  323.1 33.4 %collective-permute-start.7 = (bf16[192,896]{1,0:T(8,128)(2,1)S(1)}, bf16[192,896]{1,0:T(8,128)(2,1)S(1)}, u32[]{:S(2)}, u32[]{:S(2)}) collective-permute-start(bf16[192,896]{1,0:T(8,128)(2,1)S(1)} %constant_dynamic-slice_fusion.33), channel_id=1, source_target_pairs={{0,2},{2,0},{4,6},{6,4},{8,10},{10,8},{12,14},{14,12},{16,18},{18,... | collective-permute-start | bytes 1032200 | tf_op jit(solution)/shard_map/ppermute | solution.py:160
  328.2 62.2 %collective-permute-start.68 = (bf16[768,512]{1,0:T(8,128)(2,1)S(1)}, bf16[768,512]{1,0:T(8,128)(2,1)S(1)}, u32[]{:S(2)}, u32[]{:S(2)}) collective-permute-start(bf16[768,512]{1,0:T(8,128)(2,1)S(1)} %maximum_select_fusion.4), channel_id=1, source_target_pairs={{0,2},{2,0},{4,6},{6,4},{8,10},{10,8},{12,14},{14,12},{16,18},{18,... | collective-permute-start | bytes 2359304 | tf_op jit(solution)/shard_map/ppermute | solution.py:160
  333.5 17.9 %collective-permute-start.25 = (bf16[48,512]{1,0:T(8,128)(2,1)S(1)}, bf16[48,512]{1,0:T(8,128)(2,1)S(1)}, u32[]{:S(2)}, u32[]{:S(2)}) collective-permute-start(bf16[48,512]{1,0:T(8,128)(2,1)S(1)} %constant_dynamic-slice_fusion.23), channel_id=1, source_target_pairs={{0,2},{2,0},{4,6},{6,4},{8,10},{10,8},{12,14},{14,12},{16,18},{18,... | collective-permute-start | bytes 147464 | tf_op jit(solution)/shard_map/ppermute | solution.py:160
  334.6 45.4 %collective-permute-start.49 = (bf16[96,2304]{1,0:T(8,128)(2,1)S(1)}, bf16[96,2304]{1,0:T(8,128)(2,1)S(1)}, u32[]{:S(2)}, u32[]{:S(2)}) collective-permute-start(bf16[96,2304]{1,0:T(8,128)(2,1)S(1)} %maximum_select_fusion.10), channel_id=1, source_target_pairs={{0,2},{2,0},{4,6},{6,4},{8,10},{10,8},{12,14},{14,12},{16,18},{18,... | collective-permute-start | bytes 1327112 | tf_op jit(solution)/shard_map/ppermute | solution.py:160
  380.2 24.6 %collective-permute-start.50 = (bf16[192,2304]{1,0:T(8,128)(2,1)S(1)}, bf16[192,2304]{1,0:T(8,128)(2,1)S(1)}, u32[]{:S(2)}, u32[]{:S(2)}) collective-permute-start(bf16[192,2304]{1,0:T(8,128)(2,1)S(1)} %maximum_select_fusion.3), channel_id=1, source_target_pairs={{0,4},{2,6},{4,0},{6,2},{8,12},{10,14},{12,8},{14,10},{16,20},{18,... | collective-permute-start | bytes 2654216 | tf_op jit(solution)/shard_map/ppermute | solution.py:160
  (85 other events, 587.6 us)
